TPU v7x, 256 devices: a whole 4x4x8 slice. The times are simulated.
256 devices in a mesh: grp: 8 (over x_lo, y), ep: 32 (over z, x_hi, core).
Axes of the slice: x: 4 (x_hi: 2, x_lo: 2; x = x_hi * 2 + x_lo), y: 4, z: 8, core: 2. Of those that a mesh axis runs over, the one named last changes fastest.
Arguments:
- tokens: bfloat16 [32768, 2048], P(('grp', 'ep')), may hold values from -6 to 6
- routes: int32 [32768, 6], P(('grp', 'ep')), may hold values from 0 to 31, all different within a row; in each aligned block of 128 rows (0 to 127, 128 to 255, ...) at most 32 rows name the same one
- route_gain: float32 [32768, 6], P(('grp', 'ep')), may hold values from 0.05 to 0.6
- gate_weight: bfloat16 [32, 2048, 768], P('ep', 'grp'), may hold values from -0.125 to 0.125
- up_weight: bfloat16 [32, 2048, 768], P('ep', 'grp'), may hold values from -0.125 to 0.125
- down_weight: bfloat16 [32, 768, 2048], P('ep', None, 'grp'), may hold values from -0.21875 to 0.21875
- norm_gain: float32 [2048], replicated, may hold values from 0.25 to 1.75
- query_weight: bfloat16 [2048, 1536], P(None, 'grp'), may hold values from -0.125 to 0.125
Outputs:
- mixed: bfloat16 [32768, 2048], P(('grp', 'ep'))
- query: bfloat16 [32768, 1536], P(('grp', 'ep'))
Inputs may be any that keep to these rules, and one draw needn't show every extreme that they name: `routes`: each row names 6 different experts. Among the 128 rows of one device no expert is named by more than 32 rows, a bound that some of them reach.
All inputs are finite; a program needn't handle non-finite values.
Results may differ from a plain program's by a relative error of at most 0.0053.
Values may be sent and summed in bfloat16 or wider, within the bound.
No kernel may reach another device: no remote copies, remote signals or barrier semaphores. Data moves between devices by JAX's collectives and lax.ppermute only.
A program may use at most 128 MiB of HBM per device.

v0:
```python
import jax
import jax.numpy as jnp
from jax import lax
from jax.sharding import PartitionSpec as P


def shards(
    tokens, routes, route_gain, gate_weight, up_weight, down_weight, norm_gain, query_weight
):
    ep_count = lax.axis_size("ep")
    tok_rows = tokens.shape[0]
    width = tokens.shape[1]
    choose = routes.shape[1]
    capacity = 8 * tok_rows // ep_count
    flat = routes.reshape(-1)
    onehot = (flat[:, None] == jnp.arange(ep_count, dtype=jnp.int32)[None, :]).astype(jnp.int32)
    counted = jnp.cumsum(onehot, axis=0)
    rank = jnp.sum(onehot * (counted - 1), axis=1)
    slot = flat * capacity + rank
    repeated = jnp.repeat(tokens, choose, axis=0)
    outbound = jnp.zeros((ep_count * capacity, width), jnp.bfloat16).at[slot].set(repeated)
    arrived = lax.all_to_all(outbound, "ep", split_axis=0, concat_axis=0, tiled=True)
    gate = jnp.dot(
        arrived,
        lax.all_gather(gate_weight[0], "grp", axis=0, tiled=True),
        preferred_element_type=jnp.float32,
    )
    up = jnp.dot(
        arrived,
        lax.all_gather(up_weight[0], "grp", axis=0, tiled=True),
        preferred_element_type=jnp.float32,
    )
    hidden = (jax.nn.silu(gate) * up).astype(jnp.bfloat16)
    answers = jnp.dot(
        hidden,
        lax.all_gather(down_weight[0], "grp", axis=1, tiled=True),
        preferred_element_type=jnp.float32,
    ).astype(jnp.bfloat16)
    returned = lax.all_to_all(answers, "ep", split_axis=0, concat_axis=0, tiled=True)
    picked = returned[slot].reshape(tok_rows, choose, width).astype(jnp.float32)
    total = tokens.astype(jnp.float32) + jnp.sum(picked * route_gain[:, :, None], axis=1)
    square = jnp.mean(total * total, axis=-1, keepdims=True)
    normed = (total * lax.rsqrt(square + 1e-06) * norm_gain).astype(jnp.bfloat16)
    query = jnp.dot(
        normed,
        lax.all_gather(query_weight, "grp", axis=1, tiled=True),
        preferred_element_type=jnp.float32,
    ).astype(jnp.bfloat16)
    return (total.astype(jnp.bfloat16), query)


def solution(mesh):
    placed = (
        P(("grp", "ep"), None),
        P(("grp", "ep"), None),
        P(("grp", "ep"), None),
        P("ep", "grp", None),
        P("ep", "grp", None),
        P("ep", None, "grp"),
        P(),
        P(None, "grp"),
    )
    return jax.shard_map(
        shards,
        mesh=mesh,
        in_specs=placed,
        out_specs=(P(("grp", "ep"), None), P(("grp", "ep"), None)),
        check_vma=False,
    )
```

profile of v0, /device:TPU:24, one launch (start us, length us, event | category | flops | bytes accessed | tf_op | source)
XLA Modules:
  0.0 354.1 jit_solution(9262614193327806445)
XLA Ops:
  7.2 0.7 all-gather.12.cloned.1.call-update
  7.9 0.7 all-gather.10.cloned.1.call-update
  8.6 0.8 copy.12
  9.7 1.7 reduce-window.6
  11.5 0.3 slice_reduce_fusion
  11.8 0.7 broadcast_multiply_fusion
  12.7 3.6 %broadcast_in_dim.5 = bf16[128,6,2048]{2,1,0:T(8,128)(2,1)} broadcast(bf16[128,2048]{1,0:T(8,128)(2,1)} %param.8), dimensions={0,2} | broadcast | bytes 3670016 | tf_op jit(solution)/shard_map/broadcast_in_dim | solution.py:20
  16.4 4.9 %reshape.87 = bf16[768,2048]{1,0:T(8,128)(2,1)S(1)} reshape(bf16[128,6,2048]{2,1,0:T(8,128)(2,1)} %broadcast_in_dim.5) | data formatting | bytes 6291456 | tf_op jit(solution)/shard_map/reshape | solution.py:20
  21.4 9.4 %scatter_custom_fusion = bf16[1024,2048]{1,0:T(8,128)(2,1)} fusion(s32[768]{0:T(1024)S(1)} %fusion.17, bf16[768,2048]{1,0:T(8,128)(2,1)S(1)} %reshape.87, bf16[]{:T(256)} %constant.9.clone.1), kind=kCustom, calls=%fused_computation.11 | custom fusion | bytes 4194306 | tf_op jit(solution)/shard_map/scatter | solution.py:21
  30.8 11.4 %all-to-all-start = ((bf16[32,32,2048]{2,1,0:T(8,128)(2,1)}), bf16[32,32,2048]{2,1,0:T(8,128)(2,1)}, u32[]{:S(2)}, u32[]{:S(2)}) async-start(bf16[32,32,2048]{2,1,0:T(8,128)(2,1)} %bitcast.36), calls=%async_computation | async-start | bytes 8388608 | tf_op jit(solution)/shard_map/all_to_all | solution.py:22
  42.3 0.7 all-gather.14.cloned.1.call-update
  43.2 0.3 all-gather.8.cloned.1.call-update
  43.5 35.0 %all-gather.12.cloned.1.call-done = bf16[1,2048,768]{2,1,0:T(8,128)(2,1)} async-done(((bf16[1,256,768]{2,1,0:T(8,128)(2,1)}), bf16[1,2048,768]{2,1,0:T(8,128)(2,1)}) %all-gather.12.cloned.1.call-update) | async-done | bytes 3145744 | tf_op jit(solution)/shard_map/all_gather | solution.py:30
  78.5 60.4 %all-to-all-done = bf16[32,32,2048]{2,1,0:T(8,128)(2,1)} async-done(((bf16[32,32,2048]{2,1,0:T(8,128)(2,1)}), bf16[32,32,2048]{2,1,0:T(8,128)(2,1)}, u32[]{:S(2)}, u32[]{:S(2)}) %all-to-all-start) | async-done | bytes 4194336 | tf_op jit(solution)/shard_map/all_to_all | solution.py:22
  138.9 6.2 %fusion.1 = f32[1024,768]{1,0:T(8,128)S(1)} fusion(bf16[1024,2048]{1,0:T(8,128)(2,1)} %bitcast.2, bf16[1,2048,768]{2,1,0:T(8,128)(2,1)} %all-gather.12.cloned.1.call-done), kind=kOutput, calls=%fused_computation.5 | convolution fusion | flops 3221225472 | bytes 10485760 | tf_op jit(solution)/shard_map/dot_general | solution.py:28
  145.3 56.9 %all-gather.14.cloned.1.call-done = bf16[1,768,2048]{2,1,0:T(8,128)(2,1)} async-done(((bf16[1,768,256]{2,1,0:T(8,128)(2,1)}), bf16[1,768,2048]{2,1,0:T(8,128)(2,1)}) %all-gather.14.cloned.1.call-update) | async-done | bytes 3145744 | tf_op jit(solution)/shard_map/all_gather | solution.py:36
  202.2 12.8 %convolution_convert_fusion = bf16[1024,2048]{1,0:T(8,128)(2,1)} fusion(bf16[1,768,2048]{2,1,0:T(8,128)(2,1)} %all-gather.14.cloned.1.call-done, f32[1024,768]{1,0:T(8,128)S(1)} %fusion.1, bf16[1024,2048]{1,0:T(8,128)(2,1)} %bitcast.2, bf16[1,2048,768]{2,1,0:T(8,128)(2,1)} %all-gather.10.cloned.1.call-done), kind=kOutput, calls=%fused_computation.3 | convolution fusion | flops 6449266688 | bytes 17825792 | tf_op jit(solution)/shard_map/dot_general | solution.py:34
  215.0 10.0 %all-to-all-start.1 = ((bf16[32,32,2048]{2,1,0:T(8,128)(2,1)}), bf16[32,32,2048]{2,1,0:T(8,128)(2,1)}, u32[]{:S(2)}, u32[]{:S(2)}) async-start(bf16[32,32,2048]{2,1,0:T(8,128)(2,1)} %bitcast.37), calls=%async_computation.1 | async-start | bytes 8388608 | tf_op jit(solution)/shard_map/all_to_all | solution.py:39
  225.2 96.3 %all-to-all-done.1 = bf16[32,32,2048]{2,1,0:T(8,128)(2,1)} async-done(((bf16[32,32,2048]{2,1,0:T(8,128)(2,1)}), bf16[32,32,2048]{2,1,0:T(8,128)(2,1)}, u32[]{:S(2)}, u32[]{:S(2)}) %all-to-all-start.1) | async-done | bytes 4194336 | tf_op jit(solution)/shard_map/all_to_all | solution.py:39
  321.5 9.1 %gather_fusion = bf16[768,2048]{1,0:T(8,128)(2,1)S(1)} fusion(bf16[1024,2048]{1,0:T(8,128)(2,1)} %bitcast.7, s32[1024]{0:T(1024)S(1)} %pad_clamp_fusion), kind=kCustom, calls=%fused_computation | custom fusion | bytes 6294528 | tf_op jit(solution)/shard_map/gather | solution.py:40
  330.6 3.7 %reshape.74 = f32[128,6,2048]{2,1,0:T(8,128)} reshape(bf16[768,2048]{1,0:T(8,128)(2,1)S(1)} %gather_fusion) | data formatting | bytes 9437184 | tf_op jit(solution)/shard_map/convert_element_type | solution.py:40
  334.3 6.6 %multiply_reduce_fusion = f32[128,2048]{1,0:T(8,128)S(1)} fusion(f32[128,6,2048]{2,1,0:T(8,128)} %reshape.74, f32[128,6]{1,0:T(8,128)S(1)} %copy.15), kind=kLoop, calls=%fused_computation.2 | loop fusion | flops 2883584 | bytes 7343104 | tf_op jit(solution)/shard_map/reduce_sum | solution.py:41
  340.9 0.9 multiply_reduce_fusion.1
  341.9 5.7 %convolution_convert_fusion.1 = bf16[128,1536]{1,0:T(8,128)(2,1)} fusion(bf16[2048,1536]{0,1:T(8,128)(2,1)} %all-gather.8.cloned.1.call-done, f32[2048]{0:T(1024)S(1)} %copy-done.1, f32[128]{0:T(128)S(1)} %add_rsqrt_fusion, f32[128,2048]{1,0:T(8,128)S(1)} %multiply_reduce_fusion, bf16[128,2048]{1,0:T(8,128)(2,1)S(1)} %copy-done), kind=kOutput, calls=%fused_computation.10 | convolution fusion | flops 806813696 | bytes 8266240 | tf_op jit(solution)/shard_map/dot_general | solution.py:44
  (23 shorter events, 1.3 us)
Async XLA Ops:
  7.2 71.3 %all-gather.12.cloned.1.call-start = ((), (), s32[]{:S(2)}) async-start(), calls=%async_computation.4 | async-start | bytes 3538944 | tf_op jit(solution)/shard_map/all_gather | solution.py:30
  7.9 137.4 %all-gather.10.cloned.1.call-start = ((), (), s32[]{:S(2)}) async-start(), calls=%async_computation.3 | async-start | bytes 3538944 | tf_op jit(solution)/shard_map/all_gather | solution.py:25
  30.8 108.1 %all-to-all-start = ((bf16[32,32,2048]{2,1,0:T(8,128)(2,1)}), bf16[32,32,2048]{2,1,0:T(8,128)(2,1)}, u32[]{:S(2)}, u32[]{:S(2)}) async-start(bf16[32,32,2048]{2,1,0:T(8,128)(2,1)} %bitcast.36), calls=%async_computation | async-start | bytes 8388608 | tf_op jit(solution)/shard_map/all_to_all | solution.py:22
  42.2 160.0 %all-gather.14.cloned.1.call-start = ((), (), s32[]{:S(2)}) async-start(), calls=%async_computation.5 | async-start | bytes 3538944 | tf_op jit(solution)/shard_map/all_gather | solution.py:36
  43.0 298.9 %all-gather.8.cloned.1.call-start = ((), (), s32[]{:S(2)}) async-start(), calls=%async_computation.2 | async-start | bytes 7077888 | tf_op jit(solution)/shard_map/all_gather | solution.py:46
  215.0 10.0 %copy-start.2 = (f32[128,6]{0,1:T(8,128)S(1)}, f32[128,6]{0,1:T(8,128)}, u32[]{:S(2)}) copy-start(f32[128,6]{0,1:T(8,128)} %param.10) | copy-start | bytes 9220
  215.0 106.5 %all-to-all-start.1 = ((bf16[32,32,2048]{2,1,0:T(8,128)(2,1)}), bf16[32,32,2048]{2,1,0:T(8,128)(2,1)}, u32[]{:S(2)}, u32[]{:S(2)}) async-start(bf16[32,32,2048]{2,1,0:T(8,128)(2,1)} %bitcast.37), calls=%async_computation.1 | async-start | bytes 8388608 | tf_op jit(solution)/shard_map/all_to_all | solution.py:39
  334.3 6.6 %copy-start = (bf16[128,2048]{1,0:T(8,128)(2,1)S(1)}, bf16[128,2048]{1,0:T(8,128)(2,1)}, u32[]{:S(2)}) copy-start(bf16[128,2048]{1,0:T(8,128)(2,1)} %param.8) | copy-start | bytes 1572868
  334.3 7.6 %copy-start.1 = (f32[2048]{0:T(1024)S(1)}, f32[2048]{0:T(1024)}, u32[]{:S(2)}) copy-start(f32[2048]{0:T(1024)} %param.14) | copy-start | bytes 24580
Sparse Core Ops, SparseCore 0:
  9.8 68.6 all-gather.11
  80.3 64.9 all-gather.9
  147.0 55.1 all-gather.13
  203.9 118.1 all-gather.7
where the time goes:
time: 355 us; the launch traced here: 354 us
  waiting for transfers between devices  251 us (71%)
  local copies, waits for them, and re-layouts  32.4 us (9%)
  matrix products  24.7 us (7%)
  starting transfers between devices  21.8 us (6%)
  between operations  13.9 us (4%)
  other arithmetic  10.1 us (3%)
    all_to_all x1, waiting for transfers between devices, shards(): lax.all_to_all(answers, 'ep', split_axis=0, concat_axis=0, tiled=True)  96.3 us
    all_to_all x1, waiting for transfers between devices, shards(): lax.all_to_all(outbound, 'ep', split_axis=0, concat_axis=0, tiled=True)  60.4 us
    all_gather x1, waiting for transfers between devices, shards(): lax.all_gather(down_weight[0], 'grp', axis=1, tiled=True)  56.9 us
    all_gather x1, waiting for transfers between devices, shards(): lax.all_gather(up_weight[0], 'grp', axis=0, tiled=True)  35 us
    dot_general x1, matrix products, shards(): jnp.dot(hidden, lax.all_gather(down_weight[0], 'grp', axis=1, tiled=True)...  12.8 us
    all_to_all x1, starting transfers between devices, shards(): lax.all_to_all(outbound, 'ep', split_axis=0, concat_axis=0, tiled=True)  11.4 us
    all_to_all x1, starting transfers between devices, shards(): lax.all_to_all(answers, 'ep', split_axis=0, concat_axis=0, tiled=True)  10 us
    scatter x1, local copies, waits for them, and re-layouts, shards(): jnp.zeros((ep_count * capacity, width), jnp.bfloat16).at[slot].set(repeated)  9.4 us
  transfers between devices with their start and end apart: 6, of which 5 were waited for; matrix products, arithmetic and copies ran while one was open for 17% of the time, Pallas kernels for 0%

commit v1 on v0

--- a/solution.py
+++ b/solution.py
@@ -33,7 +33,9 @@
     hidden = (jax.nn.silu(gate) * up).astype(jnp.bfloat16)
     answers = jnp.dot(
         hidden,
-        lax.all_gather(down_weight[0], "grp", axis=1, tiled=True),
+        jnp.concatenate(
+            lax.all_to_all(jnp.stack([down_weight[0]] * lax.axis_size("grp")), "grp", 0, 0), axis=1
+        ),
         preferred_element_type=jnp.float32,
     ).astype(jnp.bfloat16)
     returned = lax.all_to_all(answers, "ep", split_axis=0, concat_axis=0, tiled=True)

time: 355 us -> 344 us (0.969)
  the two profiles are of different devices: /device:TPU:24 before, /device:TPU:2 now
where the time goes in v1:
time: 344 us; the launch traced here: 343 us
  waiting for transfers between devices  220 us (64%)
  starting transfers between devices  38.9 us (11%)
  local copies, waits for them, and re-layouts  34.4 us (10%)
  matrix products  26.3 us (8%)
  between operations  13.9 us (4%)
  other arithmetic  10.1 us (3%)
    all_to_all x1, waiting for transfers between devices, shards(): lax.all_to_all(answers, 'ep', split_axis=0, concat_axis=0, tiled=True)  96.3 us
    all_to_all x1, waiting for transfers between devices, shards(): lax.all_to_all(outbound, 'ep', split_axis=0, concat_axis=0, tiled=True)  95.8 us
    all_to_all x1, waiting for transfers between devices, shards(): lax.all_to_all(jnp.stack([down_weight[0]] * lax.axis_size('grp')), 'grp',...  25.4 us
    all_to_all x1, starting transfers between devices, shards(): lax.all_to_all(answers, 'ep', split_axis=0, concat_axis=0, tiled=True)  22.2 us
    dot_general x1, matrix products, shards(): jnp.dot(hidden, jnp.concatenate(lax.all_to_all(jnp.stack([down_weight[0]]...  12.3 us
    all_to_all x1, starting transfers between devices, shards(): lax.all_to_all(outbound, 'ep', split_axis=0, concat_axis=0, tiled=True)  10.7 us
    scatter x1, local copies, waits for them, and re-layouts, shards(): jnp.zeros((ep_count * capacity, width), jnp.bfloat16).at[slot].set(repeated)  9.4 us
    gather x1, local copies, waits for them, and re-layouts, shards(): picked = returned[slot].reshape(tok_rows, choose, width).astype(jnp.float32)  9.06 us
  transfers between devices with their start and end apart: 6, of which 3 were waited for; matrix products, arithmetic and copies ran while one was open for 19% of the time, Pallas kernels for 0%

profile of v1, /device:TPU:2, one launch (start us, length us, event | category | flops | bytes accessed | tf_op | source)
XLA Modules:
  0.0 343.3 jit_solution(17175542063401335395)
XLA Ops:
  7.2 0.7 all-gather.10.cloned.1.call-update
  7.9 0.8 copy.12
  9.0 1.7 reduce-window.6
  10.7 0.3 slice_reduce_fusion
  11.0 0.7 broadcast_multiply_fusion
  12.0 3.6 %broadcast_in_dim.5 = bf16[128,6,2048]{2,1,0:T(8,128)(2,1)} broadcast(bf16[128,2048]{1,0:T(8,128)(2,1)} %param.8), dimensions={0,2} | broadcast | bytes 3670016 | tf_op jit(solution)/shard_map/broadcast_in_dim | solution.py:20
  15.6 4.9 %reshape.96 = bf16[768,2048]{1,0:T(8,128)(2,1)S(1)} reshape(bf16[128,6,2048]{2,1,0:T(8,128)(2,1)} %broadcast_in_dim.5) | data formatting | bytes 6291456 | tf_op jit(solution)/shard_map/reshape | solution.py:20
  20.6 9.4 %scatter_custom_fusion = bf16[1024,2048]{1,0:T(8,128)(2,1)} fusion(s32[768]{0:T(1024)S(1)} %fusion.16, bf16[768,2048]{1,0:T(8,128)(2,1)S(1)} %reshape.96, bf16[]{:T(256)} %constant.9.clone.1), kind=kCustom, calls=%fused_computation.10 | custom fusion | bytes 4194306 | tf_op jit(solution)/shard_map/scatter | solution.py:21
  30.0 10.7 %all-to-all-start = ((bf16[32,32,2048]{2,1,0:T(8,128)(2,1)}), bf16[32,32,2048]{2,1,0:T(8,128)(2,1)}, u32[]{:S(2)}, u32[]{:S(2)}) async-start(bf16[32,32,2048]{2,1,0:T(8,128)(2,1)} %bitcast.38), calls=%async_computation | async-start | bytes 8388608 | tf_op jit(solution)/shard_map/all_to_all | solution.py:22
  40.8 0.7 all-gather.8.cloned.1.call-update
  41.7 95.8 %all-to-all-done = bf16[32,32,2048]{2,1,0:T(8,128)(2,1)} async-done(((bf16[32,32,2048]{2,1,0:T(8,128)(2,1)}), bf16[32,32,2048]{2,1,0:T(8,128)(2,1)}, u32[]{:S(2)}, u32[]{:S(2)}) %all-to-all-start) | async-done | bytes 4194336 | tf_op jit(solution)/shard_map/all_to_all | solution.py:22
  137.4 1.9 stack.3
  139.3 5.9 %all-to-all-start.1 = ((bf16[8,768,256]{1,2,0:T(8,128)(2,1)}), bf16[8,768,256]{1,2,0:T(8,128)(2,1)S(1)}, u32[]{:S(2)}, u32[]{:S(2)}) async-start(bf16[8,768,256]{1,2,0:T(8,128)(2,1)} %stack.3), calls=%async_computation.1 | async-start | bytes 6291456 | tf_op jit(solution)/shard_map/all_to_all | solution.py:37
  145.2 0.7 all-gather.6.cloned.1.call-update
  146.0 8.3 %fusion = f32[1024,768]{1,0:T(8,128)} fusion(bf16[1024,2048]{1,0:T(8,128)(2,1)} %bitcast.2, bf16[1,2048,768]{2,1,0:T(8,128)(2,1)} %all-gather.10.cloned.1.call-done), kind=kOutput, calls=%fused_computation.4 | convolution fusion | flops 3221225472 | bytes 10485760 | tf_op jit(solution)/shard_map/dot_general | solution.py:28
  154.2 25.4 %all-to-all-done.1 = bf16[8,768,256]{1,2,0:T(8,128)(2,1)S(1)} async-done(((bf16[8,768,256]{1,2,0:T(8,128)(2,1)}), bf16[8,768,256]{1,2,0:T(8,128)(2,1)S(1)}, u32[]{:S(2)}, u32[]{:S(2)}) %all-to-all-start.1) | async-done | bytes 3145760 | tf_op jit(solution)/shard_map/all_to_all | solution.py:37
  179.7 12.3 %convolution_convert_fusion = bf16[1024,2048]{1,0:T(8,128)(2,1)} fusion(bf16[768,2048]{0,1:T(8,128)(2,1)S(1)} %bitcast.40, f32[1024,768]{1,0:T(8,128)} %fusion, bf16[1024,2048]{1,0:T(8,128)(2,1)} %bitcast.2, bf16[1,2048,768]{2,1,0:T(8,128)(2,1)} %all-gather.8.cloned.1.call-done), kind=kOutput, calls=%fused_computation.3 | convolution fusion | flops 6449266688 | bytes 17825792 | tf_op jit(solution)/shard_map/dot_general | solution.py:34
  192.0 22.2 %all-to-all-start.2 = ((bf16[32,32,2048]{2,1,0:T(8,128)(2,1)}), bf16[32,32,2048]{2,1,0:T(8,128)(2,1)}, u32[]{:S(2)}, u32[]{:S(2)}) async-start(bf16[32,32,2048]{2,1,0:T(8,128)(2,1)} %bitcast.39), calls=%async_computation.2 | async-start | bytes 8388608 | tf_op jit(solution)/shard_map/all_to_all | solution.py:41
  214.4 96.3 %all-to-all-done.2 = bf16[32,32,2048]{2,1,0:T(8,128)(2,1)} async-done(((bf16[32,32,2048]{2,1,0:T(8,128)(2,1)}), bf16[32,32,2048]{2,1,0:T(8,128)(2,1)}, u32[]{:S(2)}, u32[]{:S(2)}) %all-to-all-start.2) | async-done | bytes 4194336 | tf_op jit(solution)/shard_map/all_to_all | solution.py:41
  310.7 9.1 %gather_fusion = bf16[768,2048]{1,0:T(8,128)(2,1)S(1)} fusion(bf16[1024,2048]{1,0:T(8,128)(2,1)} %bitcast.9, s32[1024]{0:T(1024)S(1)} %pad_clamp_fusion), kind=kCustom, calls=%fused_computation | custom fusion | bytes 6294528 | tf_op jit(solution)/shard_map/gather | solution.py:42
  319.8 3.7 %reshape.83 = f32[128,6,2048]{2,1,0:T(8,128)} reshape(bf16[768,2048]{1,0:T(8,128)(2,1)S(1)} %gather_fusion) | data formatting | bytes 9437184 | tf_op jit(solution)/shard_map/convert_element_type | solution.py:42
  323.5 6.6 %multiply_reduce_fusion = f32[128,2048]{1,0:T(8,128)S(1)} fusion(f32[128,6,2048]{2,1,0:T(8,128)} %reshape.83, f32[128,6]{1,0:T(8,128)S(1)} %copy.16), kind=kLoop, calls=%fused_computation.2 | loop fusion | flops 2883584 | bytes 7343104 | tf_op jit(solution)/shard_map/reduce_sum | solution.py:43
  330.1 0.9 multiply_reduce_fusion.1
  331.1 5.8 %convolution_convert_fusion.1 = bf16[128,1536]{1,0:T(8,128)(2,1)} fusion(bf16[2048,1536]{0,1:T(8,128)(2,1)} %all-gather.6.cloned.1.call-done, f32[2048]{0:T(1024)S(1)} %copy-done.2, f32[128]{0:T(128)S(1)} %add_rsqrt_fusion, f32[128,2048]{1,0:T(8,128)S(1)} %multiply_reduce_fusion, bf16[128,2048]{1,0:T(8,128)(2,1)S(1)} %copy-done), kind=kOutput, calls=%fused_computation.9 | convolution fusion | flops 806813696 | bytes 8266240 | tf_op jit(solution)/shard_map/dot_general | solution.py:46
  (26 shorter events, 1.1 us)
Async XLA Ops:
  7.2 138.8 %all-gather.10.cloned.1.call-start = ((), (), s32[]{:S(2)}) async-start(), calls=%async_computation.5 | async-start | bytes 3538944 | tf_op jit(solution)/shard_map/all_gather | solution.py:30
  30.0 11.4 %copy-start.1 = (bf16[1,768,256]{2,1,0:T(8,128)(2,1)S(1)}, bf16[1,768,256]{2,1,0:T(8,128)(2,1)}, u32[]{:S(2)}) copy-start(bf16[1,768,256]{2,1,0:T(8,128)(2,1)} %param.13) | copy-start | bytes 1179652
  30.0 107.4 %all-to-all-start = ((bf16[32,32,2048]{2,1,0:T(8,128)(2,1)}), bf16[32,32,2048]{2,1,0:T(8,128)(2,1)}, u32[]{:S(2)}, u32[]{:S(2)}) async-start(bf16[32,32,2048]{2,1,0:T(8,128)(2,1)} %bitcast.38), calls=%async_computation | async-start | bytes 8388608 | tf_op jit(solution)/shard_map/all_to_all | solution.py:22
  40.7 139.0 %all-gather.8.cloned.1.call-start = ((), (), s32[]{:S(2)}) async-start(), calls=%async_computation.4 | async-start | bytes 3538944 | tf_op jit(solution)/shard_map/all_gather | solution.py:25
  139.3 40.4 %all-to-all-start.1 = ((bf16[8,768,256]{1,2,0:T(8,128)(2,1)}), bf16[8,768,256]{1,2,0:T(8,128)(2,1)S(1)}, u32[]{:S(2)}, u32[]{:S(2)}) async-start(bf16[8,768,256]{1,2,0:T(8,128)(2,1)} %stack.3), calls=%async_computation.1 | async-start | bytes 6291456 | tf_op jit(solution)/shard_map/all_to_all | solution.py:37
  145.2 185.8 %all-gather.6.cloned.1.call-start = ((), (), s32[]{:S(2)}) async-start(), calls=%async_computation.3 | async-start | bytes 7077888 | tf_op jit(solution)/shard_map/all_gather | solution.py:48
  192.0 22.2 %copy-start.3 = (f32[128,6]{0,1:T(8,128)S(1)}, f32[128,6]{0,1:T(8,128)}, u32[]{:S(2)}) copy-start(f32[128,6]{0,1:T(8,128)} %param.10) | copy-start | bytes 9220
  192.0 118.7 %all-to-all-start.2 = ((bf16[32,32,2048]{2,1,0:T(8,128)(2,1)}), bf16[32,32,2048]{2,1,0:T(8,128)(2,1)}, u32[]{:S(2)}, u32[]{:S(2)}) async-start(bf16[32,32,2048]{2,1,0:T(8,128)(2,1)} %bitcast.39), calls=%async_computation.2 | async-start | bytes 8388608 | tf_op jit(solution)/shard_map/all_to_all | solution.py:41
  323.5 6.6 %copy-start = (bf16[128,2048]{1,0:T(8,128)(2,1)S(1)}, bf16[128,2048]{1,0:T(8,128)(2,1)}, u32[]{:S(2)}) copy-start(bf16[128,2048]{1,0:T(8,128)(2,1)} %param.8) | copy-start | bytes 1572868
  323.5 7.6 %copy-start.2 = (f32[2048]{0:T(1024)S(1)}, f32[2048]{0:T(1024)}, u32[]{:S(2)}) copy-start(f32[2048]{0:T(1024)} %param.14) | copy-start | bytes 24580
Sparse Core Ops, SparseCore 0:
  9.8 69.9 all-gather.9
  81.6 63.9 all-gather.7
  147.8 138.6 all-gather.5
